TPU v7x, 256 devices: a whole 4x4x8 slice. The times are simulated.
256 devices in a mesh: tm: 32 (over z_hi, x, core), chan: 4 (over y), win: 2 (over z_lo).
Axes of the slice: x: 4, y: 4, z: 8 (z_hi: 4, z_lo: 2; z = z_hi * 2 + z_lo), core: 2. Of those that a mesh axis runs over, the one named last changes fastest.
Arguments:
- inputs: bfloat16 [131072, 512], P(('win', 'tm', 'chan')), parts along dimension 0, may hold values from -24 to 24
- cotangent: float32 [131072, 512], P(('win', 'tm', 'chan')), parts along dimension 0, may hold values from -6 to 6
- w_filter: bfloat16 [3, 2, 512, 512], replicated, may hold values from -0.1875 to 0.1875
- w_gate: bfloat16 [3, 2, 512, 512], replicated, may hold values from -0.1875 to 0.1875
- w_res: bfloat16 [3, 512, 512], replicated, may hold values from -0.25 to 0.25
Outputs:
- output: bfloat16 [131072, 512], P(('win', 'tm', 'chan')), parts along dimension 0
- input_grad: float32 [131072, 512], P(('win', 'tm', 'chan')), parts along dimension 0
- filter_grad: float32 [6, 2, 512, 512], P('win', None, 'tm', 'chan'), parts along dimension 0
- gate_grad: float32 [6, 2, 512, 512], P('win', None, 'tm', 'chan'), parts along dimension 0
- res_grad: float32 [6, 512, 512], P('win', 'tm', 'chan'), parts along dimension 0
There are 2 independent parts, one for each index of `win`. A program takes and returns all parts, laid end to end along the dimension named above; an argument that names none is the same for every part. Nothing has to cross between parts.
All inputs are finite; a program needn't handle non-finite values.
Results may differ from a plain program's by a relative error of at most 0.018.
Values may be sent and summed in bfloat16 or wider, within the bound.
A program may use at most 128 MiB of HBM per device.

v0:
```python
import jax
import jax.numpy as jnp
from jax import lax
from jax.sharding import PartitionSpec as P


def passed_along(x, axis, by):
    count = lax.axis_size(axis)
    pairs = [(i, i + by) for i in range(count) if 0 <= i + by < count]
    return lax.ppermute(x, axis, pairs)


def body(inputs, cotangent, w_filter, w_gate, w_res):
    layers = w_filter.shape[0]
    width = w_filter.shape[2]
    hidden_width = w_filter.shape[3]
    stream = inputs
    saved = []
    for level in range(layers):
        hop = 2**level
        delayed = passed_along(stream, ("tm", "chan"), hop)
        paired = jnp.concatenate([delayed, stream], 1)
        filt = jnp.dot(
            paired,
            w_filter[level].reshape(2 * width, hidden_width),
            preferred_element_type=jnp.float32,
        )
        gated = jnp.dot(
            paired,
            w_gate[level].reshape(2 * width, hidden_width),
            preferred_element_type=jnp.float32,
        )
        tanh_f = jnp.tanh(filt)
        sig_g = jax.nn.sigmoid(gated)
        hidden = (tanh_f * sig_g).astype(jnp.bfloat16)
        saved.append((paired, tanh_f, sig_g, hidden))
        stream = (
            stream.astype(jnp.float32)
            + jnp.dot(hidden, w_res[level], preferred_element_type=jnp.float32)
        ).astype(jnp.bfloat16)
    adjoint = cotangent
    filter_list = [None] * layers
    gate_list = [None] * layers
    res_list = [None] * layers
    for level in reversed(range(layers)):
        hop = 2**level
        paired, tanh_f, sig_g, hidden = saved[level]
        adj_b = adjoint.astype(jnp.bfloat16)
        grad_r = jnp.einsum("th,tc->hc", hidden, adj_b, preferred_element_type=jnp.float32)
        d_hid = jnp.einsum("tc,hc->th", adj_b, w_res[level], preferred_element_type=jnp.float32)
        d_f = (d_hid * sig_g * (1.0 - tanh_f * tanh_f)).astype(jnp.bfloat16)
        d_g = (d_hid * tanh_f * sig_g * (1.0 - sig_g)).astype(jnp.bfloat16)
        grad_f = jnp.einsum("tc,th->ch", paired, d_f, preferred_element_type=jnp.float32).reshape(
            2, width, hidden_width
        )
        grad_g = jnp.einsum("tc,th->ch", paired, d_g, preferred_element_type=jnp.float32).reshape(
            2, width, hidden_width
        )
        both = jnp.einsum(
            "th,ch->tc",
            d_f,
            w_filter[level].reshape(2 * width, hidden_width),
            preferred_element_type=jnp.float32,
        ) + jnp.einsum(
            "th,ch->tc",
            d_g,
            w_gate[level].reshape(2 * width, hidden_width),
            preferred_element_type=jnp.float32,
        )
        back = both[:, :width]
        now = both[:, width:]
        back_moved = passed_along(back.astype(jnp.bfloat16), ("tm", "chan"), -hop).astype(
            back.dtype
        )
        adjoint = adjoint + now + back_moved
        grad_f, grad_g, grad_r = (
            lax.psum_scatter(
                grad_f.astype(jnp.bfloat16), "tm", scatter_dimension=1, tiled=True
            ).astype(jnp.float32),
            lax.psum_scatter(
                grad_g.astype(jnp.bfloat16), "tm", scatter_dimension=1, tiled=True
            ).astype(jnp.float32),
            lax.psum_scatter(
                grad_r.astype(jnp.bfloat16), "tm", scatter_dimension=0, tiled=True
            ).astype(jnp.float32),
        )
        grad_f, grad_g, grad_r = (
            lax.psum_scatter(
                grad_f.astype(jnp.bfloat16), "chan", scatter_dimension=2, tiled=True
            ).astype(jnp.float32),
            lax.psum_scatter(
                grad_g.astype(jnp.bfloat16), "chan", scatter_dimension=2, tiled=True
            ).astype(jnp.float32),
            lax.psum_scatter(
                grad_r.astype(jnp.bfloat16), "chan", scatter_dimension=1, tiled=True
            ).astype(jnp.float32),
        )
        filter_list[level] = grad_f
        gate_list[level] = grad_g
        res_list[level] = grad_r
    return (stream, adjoint, jnp.stack(filter_list), jnp.stack(gate_list), jnp.stack(res_list))


def solution(mesh):
    placed = (P(("win", "tm", "chan"), None), P(("win", "tm", "chan"), None), P(), P(), P())
    return jax.shard_map(
        body,
        mesh=mesh,
        in_specs=placed,
        out_specs=(
            P(("win", "tm", "chan"), None),
            P(("win", "tm", "chan"), None),
            P("win", None, "tm", "chan"),
            P("win", None, "tm", "chan"),
            P("win", "tm", "chan"),
        ),
        check_vma=False,
    )
```

profile of v0, /device:TPU:16, one launch (start us, length us, event | category | flops | bytes accessed | tf_op | source)
XLA Modules:
  0.0 1131.1 jit_solution(1743655321012133305)
XLA Ops:
  7.2 3.2 collective-permute-start
  10.4 1.3 copy.13
  11.7 2.2 fusion.36
  14.7 8.2 collective-permute-done
  23.1 0.9 fusion.8
  24.0 1.7 multiply_convert_fusion.8
  26.6 1.9 collective-permute-start.1
  28.5 14.3 %collective-permute-done.1 = bf16[512,512]{0,1:T(8,128)(2,1)S(1)} collective-permute-done((bf16[512,512]{0,1:T(8,128)(2,1)S(1)}, bf16[512,512]{0,1:T(8,128)(2,1)S(1)}, u32[]{:S(2)}, u32[]{:S(2)}) %collective-permute-start.1) | collective-permute-done | bytes 524320 | tf_op jit(solution)/shard_map/ppermute | solution.py:10
  42.8 0.9 fusion.5
  43.7 1.7 multiply_convert_fusion.7
  46.0 1.3 collective-permute-start.2
  47.8 1.0 collective-permute-done.2
  49.6 1.2 multiply_convert_fusion.4
  51.5 2.1 convolution_add_fusion.2
  53.6 1.3 slice.116
  54.9 1.3 collective-permute-start.3
  56.2 1.3 convolution_convert_fusion.6
  57.6 7.7 collective-permute-done.3
  65.3 1.6 fusion.14
  66.9 2.4 convolution_convert_fusion.7
  69.4 2.8 convolution_convert_fusion
  72.3 3.1 convolution_convert_fusion.3
  75.5 2.1 multiply_convert_fusion.2
  80.1 2.1 collective-permute-start.4
  82.1 19.5 %collective-permute-done.4 = bf16[512,512]{1,0:T(8,128)(2,1)S(1)} collective-permute-done((bf16[512,512]{1,0:T(8,128)(2,1)S(1)}, bf16[512,512]{1,0:T(8,128)(2,1)S(1)}, u32[]{:S(2)}, u32[]{:S(2)}) %collective-permute-start.4) | collective-permute-done | bytes 524320 | tf_op jit(solution)/shard_map/ppermute | solution.py:10
  102.0 1.3 convolution_convert_fusion.8
  103.5 2.7 convolution_convert_fusion.1
  106.4 3.2 convolution_convert_fusion.4
  109.6 63.0 %reduce-scatter.53.cloned.1.call-done = bf16[16,512]{1,0:T(8,128)(2,1)} async-done(((bf16[512,512]{1,0:T(8,128)(2,1)}), bf16[16,512]{1,0:T(8,128)(2,1)}) %reduce-scatter.53.cloned.1.call-update) | async-done | bytes 16400 | tf_op jit(solution)/shard_map/reduce_scatter | solution.py:83
  172.6 1.5 copy.33
  174.2 3.0 multiply_convert_fusion
  177.2 85.5 %reduce-scatter.51.cloned.1.call-done = bf16[16,512]{1,0:T(8,128)(2,1)} async-done(((bf16[512,512]{1,0:T(8,128)(2,1)}), bf16[16,512]{1,0:T(8,128)(2,1)}) %reduce-scatter.51.cloned.1.call-update) | async-done | bytes 16400 | tf_op jit(solution)/shard_map/reduce_scatter | solution.py:83
  262.7 1.5 copy.31
  264.2 3.1 convolution_convert_fusion.5
  267.4 86.2 %reduce-scatter.47.cloned.1.call-done = bf16[2,16,512]{2,1,0:T(8,128)(2,1)} async-done(((bf16[2,512,512]{2,1,0:T(8,128)(2,1)}), bf16[2,16,512]{2,1,0:T(8,128)(2,1)}) %reduce-scatter.47.cloned.1.call-update) | async-done | bytes 32784 | tf_op jit(solution)/shard_map/reduce_scatter | solution.py:80
  353.5 0.9 copy.27
  355.3 88.9 %reduce-scatter.41.cloned.1.call-done = bf16[2,16,512]{2,1,0:T(8,128)(2,1)} async-done(((bf16[2,512,512]{2,1,0:T(8,128)(2,1)}), bf16[2,16,512]{2,1,0:T(8,128)(2,1)}) %reduce-scatter.41.cloned.1.call-update) | async-done | bytes 32784 | tf_op jit(solution)/shard_map/reduce_scatter | solution.py:77
  444.2 0.9 copy.21
  446.0 88.1 %reduce-scatter.49.cloned.1.call-done = bf16[16,512]{1,0:T(8,128)(2,1)} async-done(((bf16[512,512]{1,0:T(8,128)(2,1)}), bf16[16,512]{1,0:T(8,128)(2,1)}) %reduce-scatter.49.cloned.1.call-update) | async-done | bytes 16400 | tf_op jit(solution)/shard_map/reduce_scatter | solution.py:83
  534.1 1.5 copy.29
  535.7 2.8 convolution_convert_fusion.2
  538.5 1.9 fusion.40
  541.2 0.9 slice.114
  542.1 2.5 collective-permute-start.5
  544.5 80.3 %reduce-scatter.45.cloned.1.call-done = bf16[2,16,512]{2,1,0:T(8,128)(2,1)} async-done(((bf16[2,512,512]{2,1,0:T(8,128)(2,1)}), bf16[2,16,512]{2,1,0:T(8,128)(2,1)}) %reduce-scatter.45.cloned.1.call-update) | async-done | bytes 32784 | tf_op jit(solution)/shard_map/reduce_scatter | solution.py:80
  624.8 0.9 copy.25
  626.6 89.1 %reduce-scatter.39.cloned.1.call-done = bf16[2,16,512]{2,1,0:T(8,128)(2,1)} async-done(((bf16[2,512,512]{2,1,0:T(8,128)(2,1)}), bf16[2,16,512]{2,1,0:T(8,128)(2,1)}) %reduce-scatter.39.cloned.1.call-update) | async-done | bytes 32784 | tf_op jit(solution)/shard_map/reduce_scatter | solution.py:77
  715.7 0.9 copy.19
  717.5 2.6 fusion.11
  720.1 2.0 copy.15
  722.2 15.3 %reduce-scatter.71.cloned.1.call-done = bf16[128,16]{1,0:T(8,128)(2,1)} async-done(((bf16[512,16]{1,0:T(8,128)(2,1)}), bf16[128,16]{1,0:T(8,128)(2,1)}) %reduce-scatter.71.cloned.1.call-update) | async-done | bytes 4112
  738.3 24.7 %reduce-scatter.69.cloned.1.call-done = bf16[128,16]{1,0:T(8,128)(2,1)} async-done(((bf16[512,16]{1,0:T(8,128)(2,1)}), bf16[128,16]{1,0:T(8,128)(2,1)}) %reduce-scatter.69.cloned.1.call-update) | async-done | bytes 4112
  763.8 94.1 %reduce-scatter.37.cloned.1.call-done = bf16[2,16,512]{2,1,0:T(8,128)(2,1)} async-done(((bf16[2,512,512]{2,1,0:T(8,128)(2,1)}), bf16[2,16,512]{2,1,0:T(8,128)(2,1)}) %reduce-scatter.37.cloned.1.call-update) | async-done | bytes 32784 | tf_op jit(solution)/shard_map/reduce_scatter | solution.py:77
  857.9 0.9 copy.17
  859.7 2.3 fusion.12
  862.0 17.7 %reduce-scatter.65.cloned.1.call-done = bf16[128,32]{1,0:T(8,128)(2,1)} async-done(((bf16[512,32]{1,0:T(8,128)(2,1)}), bf16[128,32]{1,0:T(8,128)(2,1)}) %reduce-scatter.65.cloned.1.call-update) | async-done | bytes 8208
  880.7 24.4 %reduce-scatter.59.cloned.1.call-done = bf16[128,32]{1,0:T(8,128)(2,1)} async-done(((bf16[512,32]{1,0:T(8,128)(2,1)}), bf16[128,32]{1,0:T(8,128)(2,1)}) %reduce-scatter.59.cloned.1.call-update) | async-done | bytes 8208
  906.0 24.6 %reduce-scatter.67.cloned.1.call-done = bf16[128,16]{1,0:T(8,128)(2,1)} async-done(((bf16[512,16]{1,0:T(8,128)(2,1)}), bf16[128,16]{1,0:T(8,128)(2,1)}) %reduce-scatter.67.cloned.1.call-update) | async-done | bytes 4112
  931.4 93.6 %reduce-scatter.43.cloned.1.call-done = bf16[2,16,512]{2,1,0:T(8,128)(2,1)} async-done(((bf16[2,512,512]{2,1,0:T(8,128)(2,1)}), bf16[2,16,512]{2,1,0:T(8,128)(2,1)}) %reduce-scatter.43.cloned.1.call-update) | async-done | bytes 32784 | tf_op jit(solution)/shard_map/reduce_scatter | solution.py:80
  1025.0 0.9 copy.23
  1027.4 19.3 %reduce-scatter.63.cloned.1.call-done = bf16[128,32]{1,0:T(8,128)(2,1)} async-done(((bf16[512,32]{1,0:T(8,128)(2,1)}), bf16[128,32]{1,0:T(8,128)(2,1)}) %reduce-scatter.63.cloned.1.call-update) | async-done | bytes 8208
  1047.6 24.4 %reduce-scatter.57.cloned.1.call-done = bf16[128,32]{1,0:T(8,128)(2,1)} async-done(((bf16[512,32]{1,0:T(8,128)(2,1)}), bf16[128,32]{1,0:T(8,128)(2,1)}) %reduce-scatter.57.cloned.1.call-update) | async-done | bytes 8208
  1073.0 24.4 %reduce-scatter.55.cloned.1.call-done = bf16[128,32]{1,0:T(8,128)(2,1)} async-done(((bf16[512,32]{1,0:T(8,128)(2,1)}), bf16[128,32]{1,0:T(8,128)(2,1)}) %reduce-scatter.55.cloned.1.call-update) | async-done | bytes 8208
  1098.3 24.4 %reduce-scatter.61.cloned.1.call-done = bf16[128,32]{1,0:T(8,128)(2,1)} async-done(((bf16[512,32]{1,0:T(8,128)(2,1)}), bf16[128,32]{1,0:T(8,128)(2,1)}) %reduce-scatter.61.cloned.1.call-update) | async-done | bytes 8208
  (139 shorter events, 23.1 us)
Async XLA Ops:
  7.2 165.5 %reduce-scatter.53.cloned.1.call-start = ((), (), s32[]{:S(2)}) async-start(), calls=%async_computation.26 | async-start | bytes 540672 | tf_op jit(solution)/shard_map/reduce_scatter | solution.py:83
  7.2 15.8 %collective-permute-start = (bf16[512,512]{1,0:T(8,128)(2,1)}, bf16[512,512]{1,0:T(8,128)(2,1)S(1)}, u32[]{:S(2)}, u32[]{:S(2)}) collective-permute-start(bf16[512,512]{1,0:T(8,128)(2,1)} %param.5), channel_id=1, source_target_pairs={{0,2},{2,4},{4,6},{6,8},{8,10},{10,12},{12,14},{14,16},{16,18},{18... | collective-permute-start | bytes 1572872 | tf_op jit(solution)/shard_map/ppermute | solution.py:10
  11.7 2.8 copy-start.9
  14.5 8.6 copy-start.3
  14.5 28.3 %copy-start.7 = (bf16[1,2,512,512]{3,2,1,0:T(8,128)(2,1)}, bf16[1,2,512,512]{3,2,1,0:T(8,128)(2,1)S(1)}, u32[]{:S(2)}) copy-start(bf16[1,2,512,512]{3,2,1,0:T(8,128)(2,1)S(1)} %get-tuple-element.23) | copy-start | bytes 3145732
  14.5 8.5 copy-start.13
  14.7 29.0 %copy-start.1 = (bf16[1,2,512,512]{3,2,1,0:T(8,128)(2,1)}, bf16[1,2,512,512]{3,2,1,0:T(8,128)(2,1)S(1)}, u32[]{:S(2)}) copy-start(bf16[1,2,512,512]{3,2,1,0:T(8,128)(2,1)S(1)} %get-tuple-element.26) | copy-start | bytes 3145732
  23.1 3.4 copy-start.10
  24.0 1.7 copy-start.5
  24.0 2.0 copy-start.19
  25.7 18.0 %copy-start.14 = (bf16[512,512]{1,0:T(8,128)(2,1)}, bf16[512,512]{1,0:T(8,128)(2,1)S(1)}, u32[]{:S(2)}) copy-start(bf16[512,512]{1,0:T(8,128)(2,1)S(1)} %get-tuple-element.28) | copy-start | bytes 1572868
  26.6 18.9 %copy-start.29 = (bf16[512,512]{0,1:T(8,128)(2,1)}, bf16[512,512]{0,1:T(8,128)(2,1)S(1)}, u32[]{:S(2)}) copy-start(bf16[512,512]{0,1:T(8,128)(2,1)S(1)} %fusion.9) | copy-start | bytes 1572868
  26.6 16.2 %collective-permute-start.1 = (bf16[512,512]{0,1:T(8,128)(2,1)S(1)}, bf16[512,512]{0,1:T(8,128)(2,1)S(1)}, u32[]{:S(2)}, u32[]{:S(2)}) collective-permute-start(bf16[512,512]{0,1:T(8,128)(2,1)S(1)} %fusion.9), channel_id=1, source_target_pairs={{0,4},{2,6},{4,8},{6,10},{8,12},{10,14},{12,16},{14,18},{16,20},{1... | collective-permute-start | bytes 1572872 | tf_op jit(solution)/shard_map/ppermute | solution.py:10
  42.8 0.9 copy-start.31
  43.7 1.7 copy-start.20
  45.4 2.3 copy-start.24
  45.4 1.8 copy-start
  45.9 3.6 copy-start.27
  46.0 2.8 collective-permute-start.2
  48.8 0.8 copy-start.32
  50.8 2.9 copy-start.22
  50.8 2.9 copy-start.25
  50.8 5.4 copy-start.23
  54.9 10.3 collective-permute-start.3
  57.5 205.1 %reduce-scatter.51.cloned.1.call-start = ((), (), s32[]{:S(2)}) async-start(), calls=%async_computation.25 | async-start | bytes 540672 | tf_op jit(solution)/shard_map/reduce_scatter | solution.py:83
  66.9 2.5 copy-start.26
  66.9 2.5 copy-start.28
  69.3 284.2 %reduce-scatter.47.cloned.1.call-start = ((), (), s32[]{:S(2)}) async-start(), calls=%async_computation.23 | async-start | bytes 1081344 | tf_op jit(solution)/shard_map/reduce_scatter | solution.py:80
  72.2 3.2 copy-start.21
  72.2 372.0 %reduce-scatter.41.cloned.1.call-start = ((), (), s32[]{:S(2)}) async-start(), calls=%async_computation.20 | async-start | bytes 1081344 | tf_op jit(solution)/shard_map/reduce_scatter | solution.py:77
  75.4 458.7 %reduce-scatter.49.cloned.1.call-start = ((), (), s32[]{:S(2)}) async-start(), calls=%async_computation.24 | async-start | bytes 540672 | tf_op jit(solution)/shard_map/reduce_scatter | solution.py:83
  75.5 2.2 copy-start.2
  77.6 0.8 copy-start.12
  77.6 2.4 copy-start.17
  77.6 1.6 copy-start.8
  80.1 21.9 %copy-start.15 = (bf16[512,512]{1,0:T(8,128)(2,1)S(1)}, bf16[512,512]{1,0:T(8,128)(2,1)}, u32[]{:S(2)}) copy-start(bf16[512,512]{1,0:T(8,128)(2,1)} %copy-done.14) | copy-start | bytes 1572868
  80.1 21.6 %collective-permute-start.4 = (bf16[512,512]{1,0:T(8,128)(2,1)S(1)}, bf16[512,512]{1,0:T(8,128)(2,1)S(1)}, u32[]{:S(2)}, u32[]{:S(2)}) collective-permute-start(bf16[512,512]{1,0:T(8,128)(2,1)S(1)} %slice.115), channel_id=1, source_target_pairs={{4,0},{6,2},{8,4},{10,6},{12,8},{14,10},{16,12},{18,14},{20,16},{2... | collective-permute-start | bytes 1572872 | tf_op jit(solution)/shard_map/ppermute | solution.py:10
  102.0 1.6 copy-start.18
  102.0 1.6 copy-start.30
  103.3 521.6 %reduce-scatter.45.cloned.1.call-start = ((), (), s32[]{:S(2)}) async-start(), calls=%async_computation.22 | async-start | bytes 1081344 | tf_op jit(solution)/shard_map/reduce_scatter | solution.py:80
  106.3 67.9 %copy-start.6 = (f32[512,512]{1,0:T(8,128)S(1)}, f32[512,512]{1,0:T(8,128)}, u32[]{:S(2)}) copy-start(f32[512,512]{1,0:T(8,128)} %copy-done.5) | copy-start | bytes 3145732
  106.3 609.4 %reduce-scatter.39.cloned.1.call-start = ((), (), s32[]{:S(2)}) async-start(), calls=%async_computation.19 | async-start | bytes 1081344 | tf_op jit(solution)/shard_map/reduce_scatter | solution.py:77
  109.5 628.0 %reduce-scatter.71.cloned.1.call-start = ((), (), s32[]{:S(2)}) async-start(), calls=%async_computation.35 | async-start | bytes 163840
  174.1 588.9 %reduce-scatter.69.cloned.1.call-start = ((), (), s32[]{:S(2)}) async-start(), calls=%async_computation.34 | async-start | bytes 163840
  264.2 593.7 %reduce-scatter.37.cloned.1.call-start = ((), (), s32[]{:S(2)}) async-start(), calls=%async_computation.18 | async-start | bytes 1081344 | tf_op jit(solution)/shard_map/reduce_scatter | solution.py:77
  267.3 268.3 %copy-start.11 = (bf16[512,1024]{1,0:T(8,128)(2,1)S(1)}, bf16[512,1024]{1,0:T(8,128)(2,1)}, u32[]{:S(2)}) copy-start(bf16[512,1024]{1,0:T(8,128)(2,1)} %copy-done.10) | copy-start | bytes 3145732
  267.3 612.4 %reduce-scatter.65.cloned.1.call-start = ((), (), s32[]{:S(2)}) async-start(), calls=%async_computation.32 | async-start | bytes 163840
  355.3 549.8 %reduce-scatter.59.cloned.1.call-start = ((), (), s32[]{:S(2)}) async-start(), calls=%async_computation.29 | async-start | bytes 163840
  446.0 484.6 %reduce-scatter.67.cloned.1.call-start = ((), (), s32[]{:S(2)}) async-start(), calls=%async_computation.33 | async-start | bytes 163840
  535.6 489.4 %reduce-scatter.43.cloned.1.call-start = ((), (), s32[]{:S(2)}) async-start(), calls=%async_computation.21 | async-start | bytes 1081344 | tf_op jit(solution)/shard_map/reduce_scatter | solution.py:80
  538.4 508.2 %reduce-scatter.63.cloned.1.call-start = ((), (), s32[]{:S(2)}) async-start(), calls=%async_computation.31 | async-start | bytes 163840
  538.5 1.9 copy-start.4
  538.5 1.9 copy-start.16
  542.1 317.7 %collective-permute-start.5 = (bf16[512,512]{1,0:T(8,128)(2,1)}, bf16[512,512]{1,0:T(8,128)(2,1)}, u32[]{:S(2)}, u32[]{:S(2)}) collective-permute-start(bf16[512,512]{1,0:T(8,128)(2,1)} %slice.114), channel_id=1, source_target_pairs={{2,0},{4,2},{6,4},{8,6},{10,8},{12,10},{14,12},{16,14},{18,16},{20... | collective-permute-start | bytes 1572872 | tf_op jit(solution)/shard_map/ppermute | solution.py:10
  626.6 445.4 %reduce-scatter.57.cloned.1.call-start = ((), (), s32[]{:S(2)}) async-start(), calls=%async_computation.28 | async-start | bytes 163840
  717.4 379.9 %reduce-scatter.55.cloned.1.call-start = ((), (), s32[]{:S(2)}) async-start(), calls=%async_computation.27 | async-start | bytes 163840
  859.7 263.0 %reduce-scatter.61.cloned.1.call-start = ((), (), s32[]{:S(2)}) async-start(), calls=%async_computation.30 | async-start | bytes 163840
Sparse Core Ops, SparseCore 0:
  57.7 114.9 reduce-scatter.52
  176.4 86.2 reduce-scatter.50
  266.5 87.0 reduce-scatter.46
  357.2 86.9 reduce-scatter.40
  447.8 86.2 reduce-scatter.48
  537.7 87.0 reduce-scatter.44
  628.6 87.0 reduce-scatter.38
  718.2 19.2 reduce-scatter.70
  740.0 22.9 reduce-scatter.68
  767.2 90.6 reduce-scatter.36
  860.4 19.2 reduce-scatter.64
  882.1 22.9 reduce-scatter.58
  907.6 22.9 reduce-scatter.66
  934.2 90.7 reduce-scatter.42
  1027.4 19.2 reduce-scatter.62
  1049.0 22.9 reduce-scatter.56
  1074.4 22.9 reduce-scatter.54
  1099.7 22.9 reduce-scatter.60
where the time goes:
time: 1130 us
  waiting for transfers between devices  1020 us (90%)
  matrix products  45.8 us (4%)
  local copies, waits for them, and re-layouts  32.7 us (3%)
  between operations  15 us (1%)
  starting transfers between devices  13.2 us (1%)
    reduce_scatter x3, waiting for transfers between devices, body(): lax.psum_scatter(grad_f.astype(jnp.bfloat16), 'tm', scatter_dimension=1,...  272 us
    reduce_scatter x3, waiting for transfers between devices, body(): lax.psum_scatter(grad_g.astype(jnp.bfloat16), 'tm', scatter_dimension=1,...  260 us
    reduce_scatter x3, waiting for transfers between devices, body(): lax.psum_scatter(grad_r.astype(jnp.bfloat16), 'tm', scatter_dimension=0,...  237 us
    unnamed x27, waiting for transfers between devices  200 us
    ppermute x6, waiting for transfers between devices, passed_along(): return lax.ppermute(x, axis, pairs)  50.7 us
    unnamed x99, local copies, waits for them, and re-layouts  28 us
  transfers between devices with their start and end apart: 24, of which 23 were waited for; matrix products, arithmetic and copies ran while one was open for 6% of the time, Pallas kernels for 0%

commit v1 on v0

v1 whole, which is shorter than its diff:
```python
import jax
import jax.numpy as jnp
from jax import lax
from jax.experimental import pallas as pl
from jax.experimental.pallas import tpu as pltpu
from jax.sharding import PartitionSpec as P

MESH = pl.DeviceIdType.MESH
MATS = 5
ROWS = 16
DEEP = MATS * ROWS
CUT = 48
RINGS = 5
F32 = jnp.float32
BF16 = jnp.bfloat16


def whereabouts():
    tm = lax.axis_index("tm")
    return tm // 8, (tm // 2) % 4, tm % 2, lax.axis_index("chan")


def device_at(z, x, core, y):
    return {"tm": z * 8 + x * 2 + core, "chan": y}


class Ring:
    def __init__(self, place, up, down, piece, slots, merged, sends, recvs):
        self.p, self.up, self.down = place, up, down
        self.piece, self.slots, self.merged = piece, slots, merged
        self.sends, self.recvs = sends, recvs
        self.next, self.last, self.far = (place + 1) % 4, (place + 3) % 4, (place + 2) % 4

    def copy(self, k, source, to):
        return pltpu.make_async_remote_copy(
            src_ref=source,
            dst_ref=self.slots[k],
            send_sem=self.sends.at[k],
            recv_sem=self.recvs.at[k],
            device_id=to,
            device_id_type=MESH,
        )

    def copies(self):
        return [
            self.copy(0, self.piece(self.far, 1), self.up),
            self.copy(1, self.piece(self.far, 0), self.down),
            self.copy(2, self.piece(self.next, 0), self.up),
            self.copy(3, self.piece(self.last, 1), self.down),
            self.copy(4, self.merged[0], self.up),
            self.copy(5, self.merged[1], self.down),
        ]

    def first(self):
        for c in self.copies()[:4]:
            c.start()

    def second(self):
        every = self.copies()
        every[0].wait_recv()
        self.merged[0][...] = add(self.slots[0][...], self.piece(self.next, 1)[...])
        every[4].start()
        every[1].wait_recv()
        self.merged[1][...] = add(self.slots[1][...], self.piece(self.last, 0)[...])
        every[5].start()

    def finish(self, store):
        every = self.copies()
        every[2].wait_recv()
        every[5].wait_recv()
        store(0, total(self.piece(self.p, 0)[...], self.slots[2][...], self.slots[5][...]))
        every[3].wait_recv()
        every[4].wait_recv()
        store(1, total(self.piece(self.p, 1)[...], self.slots[3][...], self.slots[4][...]))

    def drain(self):
        for c in self.copies():
            c.wait_send()


def add(a, b):
    return (a.astype(F32) + b.astype(F32)).astype(BF16)


def total(a, b, c):
    return a.astype(F32) + b.astype(F32) + c.astype(F32)


def ring_scratch(layers):
    wide, narrow = (2, 4, DEEP, 128), (2, DEEP, 128)
    return [
        pltpu.VMEM((layers, 4, 4, 4, DEEP, 128), BF16),
        pltpu.VMEM((layers, 4, 4, 4, DEEP, 128), BF16),
        pltpu.VMEM((layers, 2, 6, 4, DEEP, 128), BF16),
        pltpu.VMEM((layers, 2) + wide, BF16),
        pltpu.VMEM((layers, 2) + wide, BF16),
        pltpu.VMEM((layers, 2, 6, DEEP, 128), BF16),
        pltpu.VMEM((layers, 2) + narrow, BF16),
        pltpu.VMEM((layers, 4, DEEP, 128), BF16),
        pltpu.VMEM((layers, 6, CUT, 128), BF16),
        pltpu.VMEM((layers, 2, CUT, 128), BF16),
        pltpu.SemaphoreType.DMA((layers, RINGS, 6)),
        pltpu.SemaphoreType.DMA((layers, RINGS, 6)),
        pltpu.SemaphoreType.DMA((layers,)),
        pltpu.SemaphoreType.DMA((layers,)),
    ]


class Reduce:
    steps = 8

    def __init__(self, layer, grads, out, scratch):
        (other, sums, slots1, merged1, result1, slots2, merged2, result2, slots3, merged3, ring_send, ring_recv, core_send,
         core_recv) = scratch
        z, x, core, y = whereabouts()
        self.layer, self.core, self.grads, self.out = layer, core, grads, out
        self.other, self.sums, self.result1, self.result2 = other.at[layer], sums.at[layer], result1.at[layer], result2.at[layer]
        self.swap = pltpu.make_async_remote_copy(
            src_ref=grads.at[:, :, :, 1 - core],
            dst_ref=self.other,
            send_sem=core_send.at[layer],
            recv_sem=core_recv.at[layer],
            device_id=device_at(z, x, 1 - core, y),
            device_id_type=MESH,
        )
        along_x = (x, device_at(z, (x + 1) % 4, core, y), device_at(z, (x + 3) % 4, core, y))
        along_y = (y, device_at(z, x, core, (y + 1) % 4), device_at(z, x, core, (y + 3) % 4))
        along_z = (z, device_at((z + 1) % 4, x, core, y), device_at((z + 3) % 4, x, core, y))
        sems = lambda k: (ring_send.at[layer, k], ring_recv.at[layer, k])
        many = lambda ref, lead, n: [ref.at[lead + (i,)] for i in range(n)]
        s, r1, r2 = self.sums, self.result1, self.result2
        self.rings1 = [
            Ring(*along_x, lambda q, h: s.at[:, h, q], many(slots1, (layer, 0), 6), many(merged1, (layer, 0), 2), *sems(0)),
            Ring(*along_y, lambda q, h: s.at[q, 2 + h], many(slots1, (layer, 1), 6), many(merged1, (layer, 1), 2), *sems(1)),
        ]
        self.rings2 = [
            Ring(*along_y, lambda q, h: r1.at[0, h, q], many(slots2, (layer, 0), 6), many(merged2, (layer, 0), 2), *sems(2)),
            Ring(*along_x, lambda q, h: r1.at[1, h, q], many(slots2, (layer, 1), 6), many(merged2, (layer, 1), 2), *sems(3)),
        ]
        sizes = (CUT, DEEP - CUT)
        rows = lambda h: pl.ds(h * CUT, sizes[h])
        halves = (1, 0, 0, 1, 1, 0)
        self.rows = rows
        self.ring3 = Ring(
            *along_z,
            lambda q, h: r2.at[q, rows(h)],
            [slots3.at[layer, k, pl.ds(0, sizes[halves[k]])] for k in range(6)],
            [merged3.at[layer, k, pl.ds(0, sizes[1 - k])] for k in range(2)],
            *sems(4),
        )

    def step(self, k):
        if k == 0:
            self.swap.start()
        elif k == 1:
            self.swap.wait_recv()

            @pl.loop(0, 16)
            def _(i):
                a, b = i // 4, i % 4
                self.sums[a, b] = add(self.grads[a, b, :, self.core], self.other[a, b])

            for r in self.rings1:
                r.first()
        elif k == 2:
            for r in self.rings1:
                r.second()
        elif k == 3:
            for u, r in enumerate(self.rings1):

                def store(h, v, u=u):
                    self.result1[u, h] = v.astype(BF16)

                r.finish(store)
                self.rings2[u].first()
        elif k == 4:
            for r in self.rings2:
                r.second()
        elif k == 5:
            for u, r in enumerate(self.rings2):

                def store(h, v, u=u):
                    self.result2[2 * u + h] = v.astype(BF16)

                r.finish(store)
            self.ring3.first()
        elif k == 6:
            self.ring3.second()
        elif k == 7:

            def store(h, v):
                self.out[self.layer, self.rows(h)] = v

            self.ring3.finish(store)

    def drain(self):
        self.swap.wait_send()
        for r in [*self.rings1, *self.rings2, self.ring3]:
            r.drain()


def greet():
    z, x, core, y = whereabouts()
    barrier = pltpu.get_barrier_semaphore()
    friends = [device_at(z, x, 1 - core, y)]
    for by in (1, 3):
        friends += [
            device_at(z, (x + by) % 4, core, y),
            device_at(z, x, core, (y + by) % 4),
            device_at((z + by) % 4, x, core, y),
        ]
    for f in friends:
        pl.semaphore_signal(barrier, inc=1, device_id=f, device_id_type=MESH)
    pl.semaphore_wait(barrier, len(friends))


def reduce_kernel(grads_ref, out_ref, *scratch):
    layers = grads_ref.shape[0]
    greet()
    work = [Reduce(n, grads_ref.at[n], out_ref, scratch) for n in range(layers)]
    for w in work:
        w.step(0)
    for t in range(1, Reduce.steps + layers - 1):
        for n, w in enumerate(work):
            if 1 <= t - n < Reduce.steps:
                w.step(t - n)
    for w in work:
        w.drain()


def reduced(grads):
    layers = grads.shape[0]
    return pl.pallas_call(
        reduce_kernel,
        out_shape=jax.ShapeDtypeStruct((layers, DEEP, 128), F32),
        in_specs=[pl.BlockSpec(memory_space=pltpu.VMEM)],
        out_specs=pl.BlockSpec(memory_space=pltpu.VMEM),
        scratch_shapes=ring_scratch(layers),
        compiler_params=pltpu.CompilerParams(collective_id=0, has_side_effects=True, vmem_limit_bytes=48 << 20),
        name="reduce",
    )(grads)


def passed_along(x, axis, by):
    count = lax.axis_size(axis)
    pairs = [(i, i + by) for i in range(count) if 0 <= i + by < count]
    return lax.ppermute(x, axis, pairs)


def body(inputs, cotangent, w_filter, w_gate, w_res):
    layers, _, width, hidden_width = w_filter.shape
    stream = inputs
    saved = []
    for level in range(layers):
        hop = 2**level
        delayed = passed_along(stream, ("tm", "chan"), hop)
        paired = jnp.concatenate([delayed, stream], 1)
        filt = jnp.dot(paired, w_filter[level].reshape(2 * width, hidden_width), preferred_element_type=F32)
        gated = jnp.dot(paired, w_gate[level].reshape(2 * width, hidden_width), preferred_element_type=F32)
        tanh_f = jnp.tanh(filt)
        sig_g = jax.nn.sigmoid(gated)
        hidden = (tanh_f * sig_g).astype(BF16)
        saved.append((paired, tanh_f, sig_g, hidden))
        stream = (stream.astype(F32) + jnp.dot(hidden, w_res[level], preferred_element_type=F32)).astype(BF16)
    adjoint = cotangent
    grads = [None] * layers
    for level in reversed(range(layers)):
        hop = 2**level
        paired, tanh_f, sig_g, hidden = saved[level]
        adj_b = adjoint.astype(BF16)
        grad_r = jnp.einsum("th,tc->hc", hidden, adj_b, preferred_element_type=F32)
        d_hid = jnp.einsum("tc,hc->th", adj_b, w_res[level], preferred_element_type=F32)
        d_f = (d_hid * sig_g * (1.0 - tanh_f * tanh_f)).astype(BF16)
        d_g = (d_hid * tanh_f * sig_g * (1.0 - sig_g)).astype(BF16)
        grad_f = jnp.einsum("tc,th->ch", paired, d_f, preferred_element_type=F32)
        grad_g = jnp.einsum("tc,th->ch", paired, d_g, preferred_element_type=F32)
        both = jnp.einsum(
            "th,ch->tc", d_f, w_filter[level].reshape(2 * width, hidden_width), preferred_element_type=F32
        ) + jnp.einsum("th,ch->tc", d_g, w_gate[level].reshape(2 * width, hidden_width), preferred_element_type=F32)
        back = both[:, :width]
        now = both[:, width:]
        adjoint = adjoint + now + passed_along(back.astype(BF16), ("tm", "chan"), -hop).astype(F32)
        mats = jnp.concatenate([g.astype(BF16) for g in (grad_f, grad_g, grad_r)], 0)
        mats = mats.reshape(MATS, 32, ROWS, 4, 128).transpose(3, 1, 0, 2, 4)
        grads[level] = mats.reshape(4, 4, 4, 2, DEEP, 128)
    sums = reduced(jnp.stack(grads)).reshape(layers, MATS, ROWS, 128)
    return (stream, adjoint, sums[:, 0:2], sums[:, 2:4], sums[:, 4])


def solution(mesh):
    placed = (P(("win", "tm", "chan"), None), P(("win", "tm", "chan"), None), P(), P(), P())
    return jax.shard_map(
        body,
        mesh=mesh,
        in_specs=placed,
        out_specs=(
            P(("win", "tm", "chan"), None),
            P(("win", "tm", "chan"), None),
            P("win", None, "tm", "chan"),
            P("win", None, "tm", "chan"),
            P("win", "tm", "chan"),
        ),
        check_vma=False,
    )
```

time: 1130 us -> 192 us (0.17)
  waiting for transfers between devices: 1020 us -> 30.7 us
  Pallas kernels: 0 us -> 71.1 us
  matrix products: 45.8 us -> 25.6 us
  between operations: 15 us -> 1.18 us
    reduce_scatter x9 -> x0, waiting for transfers between devices: 769 us -> none  [the longest x3 272 us: body(): lax.psum_scatter(grad_f.astype(jnp.bfloat16), 'tm', scatter_dimension=1,...]
    unnamed x27 -> x0, waiting for transfers between devices: 200 us -> none
    pallas_call x0 -> x1, Pallas kernels: none -> 71.1 us  [reduced(): pl.pallas_call(reduce_kernel, out_shape=jax.ShapeDtypeStruct((layers, DEE...]
    unnamed x99 -> x69, local copies, waits for them, and re-layouts: 28 us -> 5.65 us
    reshape x0 -> x6, local copies, waits for them, and re-layouts: none -> 22.3 us  [body(): mats = mats.reshape(MATS, 32, ROWS, 4, 128).transpose(3, 1, 0, 2, 4)]
    ppermute x6, waiting for transfers between devices: 50.7 us -> 30.7 us  [passed_along(): return lax.ppermute(x, axis, pairs)]
    dot_general x15, matrix products: 31.8 us -> 14 us  [the longest x3 4.04 us: body(): jnp.einsum('tc,hc->th', adj_b, w_res[level], preferred_element_type=F32)]
  transfers between devices with their start and end apart: 24 -> 6, of which waited for: 23 -> 4; matrix products, arithmetic and copies ran while one was open for 6% -> 23% of each run, Pallas kernels for 0% -> 38%
where the time goes in v1:
time: 192 us; the launch traced here: 188 us
  Pallas kernels  71.1 us (37%)
  local copies, waits for them, and re-layouts  33.8 us (18%)
  waiting for transfers between devices  30.7 us (16%)
  matrix products  25.6 us (13%)
  other arithmetic  14.1 us (7%)
  starting transfers between devices  11.9 us (6%)
    pallas_call x1, Pallas kernels, reduced(): pl.pallas_call(reduce_kernel, out_shape=jax.ShapeDtypeStruct((layers, DEE...  71.1 us
    ppermute x6, waiting for transfers between devices, passed_along(): return lax.ppermute(x, axis, pairs)  30.7 us
    reshape x6, local copies, waits for them, and re-layouts, body(): mats = mats.reshape(MATS, 32, ROWS, 4, 128).transpose(3, 1, 0, 2, 4)  22.3 us
    ppermute x6, starting transfers between devices, passed_along(): return lax.ppermute(x, axis, pairs)  11.9 us
    unnamed x69, local copies, waits for them, and re-layouts  5.65 us
    concatenate x3, other arithmetic, body(): jnp.concatenate([g.astype(BF16) for g in (grad_f, grad_g, grad_r)], 0)  5.24 us
    add x3, other arithmetic, body(): adjoint + now  5.12 us
    dot_general x3, matrix products, body(): jnp.dot(paired, w_filter[level].reshape(2 * width, hidden_width), preferr...  4.18 us
  transfers between devices with their start and end apart: 6, of which 4 were waited for; matrix products, arithmetic and copies ran while one was open for 23% of the time, Pallas kernels for 38%

profile of v1, /device:TPU:16, one launch (start us, length us, event | category | flops | bytes accessed | tf_op | source)
XLA Modules:
  0.0 188.4 jit_solution(6359619720937418730)
XLA Ops:
  0.6 3.2 %collective-permute-start = (bf16[512,512]{1,0:T(8,128)(2,1)}, bf16[512,512]{1,0:T(8,128)(2,1)S(1)}, u32[]{:S(2)}, u32[]{:S(2)}) collective-permute-start(bf16[512,512]{1,0:T(8,128)(2,1)} %param.5), channel_id=1, source_target_pairs={{0,2},{2,4},{4,6},{6,8},{8,10},{10,12},{12,14},{14,16},{16,18},{18... | collective-permute-start | bytes 1572872 | tf_op jit(solution)/shard_map/ppermute | solution.py:247
  3.8 1.3 copy.10
  5.1 2.2 %fusion.37 = (bf16[1,2,512,512]{3,2,1,0:T(8,128)(2,1)S(1)}, bf16[1,2,512,512]{3,2,1,0:T(8,128)(2,1)S(1)}, bf16[1,2,512,512]{3,2,1,0:T(8,128)(2,1)S(1)}) fusion(bf16[3,2,512,512]{3,2,1,0:T(8,128)(2,1)} %param.7), kind=kLoop, calls=%fused_computation.82 | loop fusion | bytes 6291456 | tf_op jit(solution)/shard_map/slice | solution.py:258
  7.3 0.6 copy-done.19
  7.9 0.4 fusion.36
  8.3 8.1 %collective-permute-done = bf16[512,512]{1,0:T(8,128)(2,1)S(1)} collective-permute-done((bf16[512,512]{1,0:T(8,128)(2,1)}, bf16[512,512]{1,0:T(8,128)(2,1)S(1)}, u32[]{:S(2)}, u32[]{:S(2)}) %collective-permute-start) | collective-permute-done | bytes 524320 | tf_op jit(solution)/shard_map/ppermute | solution.py:247
  16.6 0.9 fusion.8
  17.6 1.7 multiply_convert_fusion.8
  19.3 0.5 fusion.9
  19.8 1.9 %collective-permute-start.1 = (bf16[512,512]{0,1:T(8,128)(2,1)S(1)}, bf16[512,512]{0,1:T(8,128)(2,1)S(1)}, u32[]{:S(2)}, u32[]{:S(2)}) collective-permute-start(bf16[512,512]{0,1:T(8,128)(2,1)S(1)} %fusion.9), channel_id=1, source_target_pairs={{0,4},{2,6},{4,8},{6,10},{8,12},{10,14},{12,16},{14,18},{16,20},{1... | collective-permute-start | bytes 1572872 | tf_op jit(solution)/shard_map/ppermute | solution.py:247
  21.7 14.3 %collective-permute-done.1 = bf16[512,512]{0,1:T(8,128)(2,1)S(1)} collective-permute-done((bf16[512,512]{0,1:T(8,128)(2,1)S(1)}, bf16[512,512]{0,1:T(8,128)(2,1)S(1)}, u32[]{:S(2)}, u32[]{:S(2)}) %collective-permute-start.1) | collective-permute-done | bytes 524320 | tf_op jit(solution)/shard_map/ppermute | solution.py:247
  36.0 0.9 fusion.5
  36.9 1.7 multiply_convert_fusion.7
  38.7 0.5 fusion.10
  39.2 1.3 collective-permute-start.2
  40.5 0.5 fusion.15
  41.0 1.0 collective-permute-done.2
  42.0 0.8 convolution_tanh_fusion
  42.7 1.2 multiply_convert_fusion.4
  43.9 0.5 fusion.11
  44.4 1.3 convolution_convert_fusion.6
  45.7 0.7 fusion.39
  46.4 0.8 convolution_add_fusion.2
  47.2 0.9 slice.132
  48.2 1.5 collective-permute-start.3
  49.6 1.7 convolution_convert_fusion
  51.3 1.7 convolution_convert_fusion.1
  53.0 1.0 copy.16
  54.0 1.9 pad_maximum_fusion.3
  55.9 2.8 %reshape.24 = bf16[5,32,16,4,128]{4,3,2,1,0:T(4,128)(2,1)} reshape(bf16[2560,512]{1,0:T(8,128)(2,1)S(1)} %pad_maximum_fusion.3) | data formatting | bytes 5242880 | tf_op jit(solution)/shard_map/reshape | solution.py:284
  58.8 3.7 %copy.14 = bf16[5,32,16,4,128]{4,2,0,1,3:T(8,128)(2,1)} copy(bf16[5,32,16,4,128]{4,3,2,1,0:T(4,128)(2,1)} %reshape.24) | data formatting | bytes 5242880 | tf_op jit(solution)/shard_map/reshape | solution.py:284
  62.5 1.5 fusion.14
  64.0 0.5 convolution_convert_fusion.7
  64.5 1.8 multiply_convert_fusion.2
  66.3 0.7 fusion.40
  67.1 0.5 copy-done.18
  67.6 0.7 convolution_add_fusion.1
  68.4 1.9 %collective-permute-start.4 = (bf16[512,512]{1,0:T(8,128)(2,1)S(1)}, bf16[512,512]{1,0:T(8,128)(2,1)}, u32[]{:S(2)}, u32[]{:S(2)}) collective-permute-start(bf16[512,512]{1,0:T(8,128)(2,1)S(1)} %slice.131), channel_id=1, source_target_pairs={{4,0},{6,2},{8,4},{10,6},{12,8},{14,10},{16,12},{18,14},{20,16},{2... | collective-permute-start | bytes 1572872 | tf_op jit(solution)/shard_map/ppermute | solution.py:247
  70.3 0.7 convolution_convert_fusion.2
  71.1 0.7 convolution_convert_fusion.3
  71.8 1.7 pad_maximum_fusion.2
  73.5 4.9 %reshape.23 = bf16[5,32,16,4,128]{4,3,2,1,0:T(4,128)(2,1)} reshape(bf16[2560,512]{1,0:T(8,128)(2,1)} %pad_maximum_fusion.2) | data formatting | bytes 5242880 | tf_op jit(solution)/shard_map/reshape | solution.py:284
  78.4 3.7 %copy.13 = bf16[5,32,16,4,128]{4,2,0,1,3:T(8,128)(2,1)} copy(bf16[5,32,16,4,128]{4,3,2,1,0:T(4,128)(2,1)} %reshape.23) | data formatting | bytes 5242880 | tf_op jit(solution)/shard_map/reshape | solution.py:284
  82.1 7.4 %collective-permute-done.4 = bf16[512,512]{1,0:T(8,128)(2,1)} collective-permute-done((bf16[512,512]{1,0:T(8,128)(2,1)S(1)}, bf16[512,512]{1,0:T(8,128)(2,1)}, u32[]{:S(2)}, u32[]{:S(2)}) %collective-permute-start.4) | collective-permute-done | bytes 524320 | tf_op jit(solution)/shard_map/ppermute | solution.py:247
  89.5 1.3 fusion.13
  90.9 0.5 convolution_convert_fusion.8
  91.4 1.8 multiply_convert_fusion
  93.2 0.7 fusion.41
  93.9 0.5 copy-done.21
  94.4 0.8 convolution_convert_fusion.5
  95.2 0.8 convolution_convert_fusion.4
  95.9 0.5 copy-done.13
  96.4 0.7 convolution_add_fusion
  97.1 0.9 slice.130
  98.0 2.1 %collective-permute-start.5 = (bf16[512,512]{1,0:T(8,128)(2,1)}, bf16[512,512]{1,0:T(8,128)(2,1)}, u32[]{:S(2)}, u32[]{:S(2)}) collective-permute-start(bf16[512,512]{1,0:T(8,128)(2,1)} %slice.130), channel_id=1, source_target_pairs={{2,0},{4,2},{6,4},{8,6},{10,8},{12,10},{14,12},{16,14},{18,16},{20... | collective-permute-start | bytes 1572872 | tf_op jit(solution)/shard_map/ppermute | solution.py:247
  100.1 1.7 pad_maximum_fusion.1
  101.8 4.9 %reshape.22 = bf16[5,32,16,4,128]{4,3,2,1,0:T(4,128)(2,1)} reshape(bf16[2560,512]{1,0:T(8,128)(2,1)} %pad_maximum_fusion.1) | data formatting | bytes 5242880 | tf_op jit(solution)/shard_map/reshape | solution.py:284
  106.7 2.2 %copy.12 = bf16[5,32,16,4,128]{4,2,0,1,3:T(8,128)(2,1)S(1)} copy(bf16[5,32,16,4,128]{4,3,2,1,0:T(4,128)(2,1)} %reshape.22) | data formatting | bytes 5242880 | tf_op jit(solution)/shard_map/reshape | solution.py:284
  109.2 0.8 copy-done.1
  110.0 3.7 %pad_maximum_fusion.grads_ref = bf16[3,4,4,4,2,80,128]{6,5,4,3,2,1,0:T(8,128)(2,1)} fusion(bf16[1,4,4,4,2,80,128]{6,5,4,3,2,1,0:T(8,128)(2,1)S(1)} %bitcast.75, bf16[1,4,4,4,2,80,128]{6,5,4,3,2,1,0:T(8,128)(2,1)S(1)} %bitcast.76, bf16[1,4,4,4,2,80,128]{6,5,4,3,2,1,0:T(8,128)(2,1)S(1)} %bitcast.77), kind=kLoop, calls=%fused_computation | loop fusion | flops 7864320 | bytes 15728640 | tf_op jit(solution)/shard_map/stack | solution.py:286
  113.8 71.1 %reduce.1 = f32[3,80,128]{2,1,0:T(8,128)S(1)} custom-call(bf16[3,4,4,4,2,80,128]{6,5,4,3,2,1,0:T(8,128)(2,1)} %pad_maximum_fusion.grads_ref), custom_call_target="tpu_custom_call" | custom-call | tf_op jit(solution)/shard_map/reduce/pallas_call | solution.py:233
  184.9 0.6 slice_bitcast_fusion
  185.5 0.6 fusion.38
  186.1 2.3 %fusion.12 = f32[512,512]{1,0:T(8,128)} fusion(f32[512,512]{1,0:T(8,128)S(1)} %fusion.13, f32[512,1024]{1,0:T(8,128)S(1)} %convolution_add_fusion, bf16[512,512]{1,0:T(8,128)(2,1)} %collective-permute-done.5), kind=kLoop, calls=%fused_computation.39 | loop fusion | flops 786432 | bytes 3670016 | tf_op jit(solution)/shard_map/add | solution.py:282
  (66 shorter events, 0.7 us)
Async XLA Ops:
  0.6 15.8 %collective-permute-start = (bf16[512,512]{1,0:T(8,128)(2,1)}, bf16[512,512]{1,0:T(8,128)(2,1)S(1)}, u32[]{:S(2)}, u32[]{:S(2)}) collective-permute-start(bf16[512,512]{1,0:T(8,128)(2,1)} %param.5), channel_id=1, source_target_pairs={{0,2},{2,4},{4,6},{6,8},{8,10},{10,12},{12,14},{14,16},{16,18},{18... | collective-permute-start | bytes 1572872 | tf_op jit(solution)/shard_map/ppermute | solution.py:247
  5.1 2.8 %copy-start.19 = (bf16[3,2,512,512]{3,2,1,0:T(8,128)(2,1)S(1)}, bf16[3,2,512,512]{3,2,1,0:T(8,128)(2,1)}, u32[]{:S(2)}) copy-start(bf16[3,2,512,512]{3,2,1,0:T(8,128)(2,1)} %param.8) | copy-start | bytes 9437188
  7.9 9.5 %copy-start.4 = (bf16[1,2,512,512]{3,2,1,0:T(8,128)(2,1)}, bf16[1,2,512,512]{3,2,1,0:T(8,128)(2,1)S(1)}, u32[]{:S(2)}) copy-start(bf16[1,2,512,512]{3,2,1,0:T(8,128)(2,1)S(1)} %get-tuple-element.19) | copy-start | bytes 3145732
  7.9 29.0 %copy-start.10 = (bf16[1,2,512,512]{3,2,1,0:T(8,128)(2,1)}, bf16[1,2,512,512]{3,2,1,0:T(8,128)(2,1)S(1)}, u32[]{:S(2)}) copy-start(bf16[1,2,512,512]{3,2,1,0:T(8,128)(2,1)S(1)} %get-tuple-element.21) | copy-start | bytes 3145732
  7.9 8.5 %copy-start.22 = (bf16[512,512]{1,0:T(8,128)(2,1)S(1)}, bf16[512,512]{1,0:T(8,128)(2,1)}, u32[]{:S(2)}) copy-start(bf16[512,512]{1,0:T(8,128)(2,1)} %param.5) | copy-start | bytes 1572868
  8.3 9.1 %copy-start.12 = (bf16[1,2,512,512]{3,2,1,0:T(8,128)(2,1)}, bf16[1,2,512,512]{3,2,1,0:T(8,128)(2,1)S(1)}, u32[]{:S(2)}) copy-start(bf16[1,2,512,512]{3,2,1,0:T(8,128)(2,1)S(1)} %get-tuple-element.17) | copy-start | bytes 3145732
  8.3 27.7 %copy-start.17 = (bf16[1,2,512,512]{3,2,1,0:T(8,128)(2,1)}, bf16[1,2,512,512]{3,2,1,0:T(8,128)(2,1)S(1)}, u32[]{:S(2)}) copy-start(bf16[1,2,512,512]{3,2,1,0:T(8,128)(2,1)S(1)} %get-tuple-element.18) | copy-start | bytes 3145732
  16.5 1.1 copy-start.20
  17.4 1.9 copy-start.14
  17.6 1.7 copy-start.23
  19.8 18.9 %copy-start.29 = (bf16[512,512]{0,1:T(8,128)(2,1)}, bf16[512,512]{0,1:T(8,128)(2,1)S(1)}, u32[]{:S(2)}) copy-start(bf16[512,512]{0,1:T(8,128)(2,1)S(1)} %fusion.9) | copy-start | bytes 1572868
  19.8 16.2 %collective-permute-start.1 = (bf16[512,512]{0,1:T(8,128)(2,1)S(1)}, bf16[512,512]{0,1:T(8,128)(2,1)S(1)}, u32[]{:S(2)}, u32[]{:S(2)}) collective-permute-start(bf16[512,512]{0,1:T(8,128)(2,1)S(1)} %fusion.9), channel_id=1, source_target_pairs={{0,4},{2,6},{4,8},{6,10},{8,12},{10,14},{12,16},{14,18},{16,20},{1... | collective-permute-start | bytes 1572872 | tf_op jit(solution)/shard_map/ppermute | solution.py:247
  36.0 0.9 copy-start.31
  36.9 1.8 copy-start.24
  38.7 2.3 %copy-start.27 = (bf16[512,512]{1,0:T(8,128)(2,1)}, bf16[512,512]{1,0:T(8,128)(2,1)S(1)}, u32[]{:S(2)}) copy-start(bf16[512,512]{1,0:T(8,128)(2,1)S(1)} %get-tuple-element.27) | copy-start | bytes 1572868
  38.7 1.8 copy-start.2
  39.2 2.8 %collective-permute-start.2 = (bf16[512,512]{0,1:T(8,128)(2,1)S(1)}, bf16[512,512]{0,1:T(8,128)(2,1)S(1)}, u32[]{:S(2)}, u32[]{:S(2)}) collective-permute-start(bf16[512,512]{0,1:T(8,128)(2,1)S(1)} %fusion.10), channel_id=1, source_target_pairs={{0,8},{2,10},{4,12},{6,14},{8,16},{10,18},{12,20},{14,22},{16,24},... | collective-permute-start | bytes 1572872 | tf_op jit(solution)/shard_map/ppermute | solution.py:247
  47.2 4.1 %copy-start.6 = (f32[512,1024]{1,0:T(8,128)}, f32[512,1024]{1,0:T(8,128)S(1)}, u32[]{:S(2)}) copy-start(f32[512,1024]{1,0:T(8,128)S(1)} %convolution_add_fusion.2) | copy-start | bytes 6291460
  48.2 14.3 %collective-permute-start.3 = (bf16[512,512]{1,0:T(8,128)(2,1)}, bf16[512,512]{1,0:T(8,128)(2,1)}, u32[]{:S(2)}, u32[]{:S(2)}) collective-permute-start(bf16[512,512]{1,0:T(8,128)(2,1)} %slice.132), channel_id=1, source_target_pairs={{8,0},{10,2},{12,4},{14,6},{16,8},{18,10},{20,12},{22,14},{24,16},... | collective-permute-start | bytes 1572872 | tf_op jit(solution)/shard_map/ppermute | solution.py:247
  58.7 3.7 %copy-start.3 = (f32[512,512]{1,0:T(8,128)S(1)}, f32[512,512]{1,0:T(8,128)}, u32[]{:S(2)}) copy-start(f32[512,512]{1,0:T(8,128)} %param.6) | copy-start | bytes 3145732
  58.7 3.7 %copy-start.7 = (f32[512,1024]{1,0:T(8,128)S(1)}, f32[512,1024]{1,0:T(8,128)}, u32[]{:S(2)}) copy-start(f32[512,1024]{1,0:T(8,128)} %copy-done.6) | copy-start | bytes 6291460
  62.5 1.5 copy-start.28
  62.5 2.0 %copy-start.25 = (f32[512,512]{1,0:T(8,128)S(1)}, f32[512,512]{1,0:T(8,128)}, u32[]{:S(2)}) copy-start(f32[512,512]{1,0:T(8,128)} %copy-done.24) | copy-start | bytes 3145732
  62.5 2.1 %copy-start.26 = (f32[512,512]{1,0:T(8,128)S(1)}, f32[512,512]{1,0:T(8,128)}, u32[]{:S(2)}) copy-start(f32[512,512]{1,0:T(8,128)} %get-tuple-element.28) | copy-start | bytes 3145732
  64.5 1.8 copy-start.11
  66.3 1.2 copy-start.18
  67.5 2.8 %copy-start.30 = (bf16[512,512]{0,1:T(8,128)(2,1)S(1)}, bf16[512,512]{0,1:T(8,128)(2,1)}, u32[]{:S(2)}) copy-start(bf16[512,512]{0,1:T(8,128)(2,1)} %copy-done.29) | copy-start | bytes 1572868
  67.5 2.8 %copy-start.32 = (bf16[512,512]{0,1:T(8,128)(2,1)S(1)}, bf16[512,512]{0,1:T(8,128)(2,1)}, u32[]{:S(2)}) copy-start(bf16[512,512]{0,1:T(8,128)(2,1)} %copy-done.31) | copy-start | bytes 1572868
  68.3 2.7 %copy-start.8 = (f32[512,1024]{1,0:T(8,128)}, f32[512,1024]{1,0:T(8,128)S(1)}, u32[]{:S(2)}) copy-start(f32[512,1024]{1,0:T(8,128)S(1)} %convolution_add_fusion.1) | copy-start | bytes 6291460
  68.4 21.1 %collective-permute-start.4 = (bf16[512,512]{1,0:T(8,128)(2,1)S(1)}, bf16[512,512]{1,0:T(8,128)(2,1)}, u32[]{:S(2)}, u32[]{:S(2)}) collective-permute-start(bf16[512,512]{1,0:T(8,128)(2,1)S(1)} %slice.131), channel_id=1, source_target_pairs={{4,0},{6,2},{8,4},{10,6},{12,8},{14,10},{16,12},{18,14},{20,16},{2... | collective-permute-start | bytes 1572872 | tf_op jit(solution)/shard_map/ppermute | solution.py:247
  78.4 11.2 %copy-start.9 = (f32[512,1024]{1,0:T(8,128)S(1)}, f32[512,1024]{1,0:T(8,128)}, u32[]{:S(2)}) copy-start(f32[512,1024]{1,0:T(8,128)} %copy-done.8) | copy-start | bytes 6291460
  82.1 9.2 %copy-start.15 = (f32[512,512]{1,0:T(8,128)S(1)}, f32[512,512]{1,0:T(8,128)}, u32[]{:S(2)}) copy-start(f32[512,512]{1,0:T(8,128)} %copy-done.14) | copy-start | bytes 3145732
  82.1 9.2 %copy-start.16 = (f32[512,512]{1,0:T(8,128)S(1)}, f32[512,512]{1,0:T(8,128)}, u32[]{:S(2)}) copy-start(f32[512,512]{1,0:T(8,128)} %get-tuple-element.26) | copy-start | bytes 3145732
  91.4 1.8 copy-start.5
  93.2 1.2 copy-start.21
  95.2 1.2 copy-start.13
  98.0 88.1 %collective-permute-start.5 = (bf16[512,512]{1,0:T(8,128)(2,1)}, bf16[512,512]{1,0:T(8,128)(2,1)}, u32[]{:S(2)}, u32[]{:S(2)}) collective-permute-start(bf16[512,512]{1,0:T(8,128)(2,1)} %slice.130), channel_id=1, source_target_pairs={{2,0},{4,2},{6,4},{8,6},{10,8},{12,10},{14,12},{16,14},{18,16},{20... | collective-permute-start | bytes 1572872 | tf_op jit(solution)/shard_map/ppermute | solution.py:247
  106.7 2.5 %copy-start = (bf16[5,32,16,4,128]{4,2,0,1,3:T(8,128)(2,1)S(1)}, bf16[5,32,16,4,128]{4,2,0,1,3:T(8,128)(2,1)}, u32[]{:S(2)}) copy-start(bf16[5,32,16,4,128]{4,2,0,1,3:T(8,128)(2,1)} %copy.14) | copy-start | bytes 7864324
  106.7 3.3 %copy-start.1 = (bf16[5,32,16,4,128]{4,2,0,1,3:T(8,128)(2,1)S(1)}, bf16[5,32,16,4,128]{4,2,0,1,3:T(8,128)(2,1)}, u32[]{:S(2)}) copy-start(bf16[5,32,16,4,128]{4,2,0,1,3:T(8,128)(2,1)} %copy.13) | copy-start | bytes 7864324

commit v2 on v0

v2 whole, which is shorter than its diff:
```python
import jax
import jax.numpy as jnp
from jax import lax
from jax.experimental import pallas as pl
from jax.experimental.pallas import tpu as pltpu
from jax.sharding import PartitionSpec as P

MESH = pl.DeviceIdType.MESH
F32 = jnp.float32
BF16 = jnp.bfloat16
LAYERS = 3
C = 512
PART = 128
STREAMS = 2
R = PART // STREAMS
ROWS = 4 * R
MATS = 5
DEEP = MATS * 16
NT = 256


def whereabouts():
    tm = lax.axis_index("tm")
    return tm // 8, (tm // 2) % 4, tm % 2, lax.axis_index("chan")


def device_at(z, x, core, y):
    return {"tm": z * 8 + x * 2 + core, "chan": y}


def send(source, target, send_sem, recv_sem, to):
    return pltpu.make_async_remote_copy(
        src_ref=source, dst_ref=target, send_sem=send_sem, recv_sem=recv_sem, device_id=to, device_id_type=MESH
    )


def greet():
    z, x, core, y = whereabouts()
    tm = lax.axis_index("tm")
    barrier = pltpu.get_barrier_semaphore()
    friends = [device_at(z, x, 1 - core, y), {"tm": (tm + 1) % 32, "chan": y}, {"tm": (tm + 31) % 32, "chan": y}]
    for by in (1, 2, 3):
        friends += [
            device_at(z, (x + by) % 4, core, y),
            device_at(z, x, core, (y + by) % 4),
            device_at((z + by) % 4, x, core, y),
        ]
    for f in friends:
        pl.semaphore_signal(barrier, inc=1, device_id=f, device_id_type=MESH)
    pl.semaphore_wait(barrier, len(friends))


def dot(a, b):
    return jnp.dot(a, b, preferred_element_type=F32)


def dot_nt(a, b):
    return lax.dot_general(a, b, (((1,), (1,)), ((), ())), preferred_element_type=F32)


def total(first, *more):
    first = first.astype(F32)
    for m in more:
        first = first + m.astype(F32)
    return first


class Reduce:
    def __init__(self, layer, grads, out, s):
        z, x, core, y = whereabouts()
        self.layer, self.core, self.x, self.y, self.z = layer, core, x, y, z
        self.grads, self.out = grads.at[layer], out
        self.other, self.sums = s["other"].at[layer], s["sums"].at[layer]
        self.half, self.last = s["half"].at[layer], s["last"].at[layer]
        self.slots_x, self.slots_y = s["slots_x"].at[layer], s["slots_y"].at[layer]
        self.slots2, self.slots3 = s["slots2"].at[layer], s["slots3"].at[layer]
        self.swap = send(
            self.grads.at[:, :, :, 1 - core], self.other, s["swap_send"].at[layer], s["swap_recv"].at[layer],
            device_at(z, x, 1 - core, y),
        )
        sems = lambda k, i: (s["ring_send"].at[layer, k, i], s["ring_recv"].at[layer, k, i])
        self.copies = [[], [], [], [], []]
        for i in range(3):
            qx, qy, qz = (x + i + 1) % 4, (y + i + 1) % 4, (z + i + 1) % 4
            to_x, to_y, to_z = device_at(z, qx, core, y), device_at(z, x, core, qy), device_at(qz, x, core, y)
            for k, source, slot, to in (
                (0, self.sums.at[:, 0:2, qx], self.slots_x.at[i], to_x),
                (1, self.sums.at[qy, 2:4], self.slots_y.at[i], to_y),
                (2, self.half.at[0, qy], self.slots2.at[0, i], to_y),
                (3, self.half.at[1, qx], self.slots2.at[1, i], to_x),
                (4, self.last.at[qz], self.slots3.at[i], to_z),
            ):
                self.copies[k].append(send(source, slot, *sems(k, i), to))

    def start(self, k):
        for c in self.copies[k]:
            c.start()

    def arrived(self, k):
        for c in self.copies[k]:
            c.wait_recv()

    def step(self, k):
        if k == 0:
            self.swap.start()
        elif k == 1:
            self.swap.wait_recv()

            @pl.loop(0, 4)
            def _(a):
                self.sums[a, 0:2] = total(self.grads[a, 0:2, :, self.core], self.other[a, 0:2]).astype(BF16)

            self.start(0)

            @pl.loop(0, 4)
            def _(a):
                self.sums[a, 2:4] = total(self.grads[a, 2:4, :, self.core], self.other[a, 2:4]).astype(BF16)

            self.start(1)
        elif k == 2:
            self.arrived(0)

            @pl.loop(0, 4)
            def _(a):
                self.half[0, a] = total(self.sums[a, 0:2, self.x], *[self.slots_x[i, a] for i in range(3)]).astype(BF16)

            self.start(2)
            self.arrived(1)

            @pl.loop(0, 4)
            def _(a):
                self.half[1, a] = total(self.sums[self.y, 2:4, a], *[self.slots_y[i, :, a] for i in range(3)]).astype(BF16)

            self.start(3)
        elif k == 3:
            self.arrived(2)
            self.last[0:2] = total(self.half[0, self.y], *[self.slots2[0, i] for i in range(3)]).astype(BF16)
            self.arrived(3)
            self.last[2:4] = total(self.half[1, self.x], *[self.slots2[1, i] for i in range(3)]).astype(BF16)
            self.start(4)
        elif k == 4:
            self.arrived(4)
            self.out[self.layer] = total(self.last[self.z], *[self.slots3[i] for i in range(3)])

    def drain(self):
        self.swap.wait_send()
        for k in range(5):
            for c in self.copies[k]:
                c.wait_send()


SCRATCH = dict(
    acts=pltpu.VMEM((LAYERS, STREAMS, 8, R, C), BF16),
    final=pltpu.VMEM((STREAMS, 4, R, C), BF16),
    pre_f=pltpu.VMEM((STREAMS, ROWS, C), F32),
    pre_g=pltpu.VMEM((STREAMS, ROWS, C), F32),
    coef_f=pltpu.VMEM((LAYERS, STREAMS, ROWS, C), F32),
    coef_g=pltpu.VMEM((LAYERS, STREAMS, ROWS, C), F32),
    hidden=pltpu.VMEM((LAYERS, STREAMS, ROWS, C), BF16),
    cot=pltpu.VMEM((C, C), F32),
    cot_b=pltpu.VMEM((C, C), BF16),
    top=pltpu.VMEM((STREAMS, 4, R, C), BF16),
    adj=pltpu.VMEM((STREAMS, ROWS, C), BF16),
    gain=pltpu.VMEM((STREAMS, ROWS, C), F32),
    gain_b=pltpu.VMEM((STREAMS, 4, R, C), BF16),
    dfg=pltpu.VMEM((2, STREAMS, ROWS, C), BF16),
    back=pltpu.VMEM((LAYERS, STREAMS, 8, R, C), BF16),
    flip=pltpu.VMEM((3, C, 4 * PART), BF16),
    wf=pltpu.VMEM((LAYERS, 2, C, C), BF16),
    wg=pltpu.VMEM((LAYERS, 2, C, C), BF16),
    wr=pltpu.VMEM((LAYERS, C, C), BF16),
    grads=pltpu.VMEM((LAYERS, 4, 4, 4, 2, DEEP, 128), BF16),
    other=pltpu.VMEM((LAYERS, 4, 4, 4, DEEP, 128), BF16),
    sums=pltpu.VMEM((LAYERS, 4, 4, 4, DEEP, 128), BF16),
    slots_x=pltpu.VMEM((LAYERS, 3, 4, 2, DEEP, 128), BF16),
    slots_y=pltpu.VMEM((LAYERS, 3, 2, 4, DEEP, 128), BF16),
    half=pltpu.VMEM((LAYERS, 2, 4, 2, DEEP, 128), BF16),
    slots2=pltpu.VMEM((LAYERS, 2, 3, 2, DEEP, 128), BF16),
    last=pltpu.VMEM((LAYERS, 4, DEEP, 128), BF16),
    slots3=pltpu.VMEM((LAYERS, 3, DEEP, 128), BF16),
    ring_send=pltpu.SemaphoreType.DMA((LAYERS, 5, 3)),
    ring_recv=pltpu.SemaphoreType.DMA((LAYERS, 5, 3)),
    swap_send=pltpu.SemaphoreType.DMA((LAYERS,)),
    swap_recv=pltpu.SemaphoreType.DMA((LAYERS,)),
    load=pltpu.SemaphoreType.DMA((10,)),
    local=pltpu.SemaphoreType.DMA((4, STREAMS)),
    move_send=pltpu.SemaphoreType.DMA((4, STREAMS, 3)),
    move_recv=pltpu.SemaphoreType.DMA((4, STREAMS, 3)),
    halo_send=pltpu.SemaphoreType.DMA((2, LAYERS, STREAMS)),
    halo_recv=pltpu.SemaphoreType.DMA((2, LAYERS, STREAMS)),
)


def pass_kernel(x_ref, c_ref, wf_ref, wg_ref, wr_ref, y_ref, gain_ref, out_ref, *scratch):
    s = dict(zip(SCRATCH, scratch))
    acts, back, grads = s["acts"], s["back"], s["grads"]
    z, x, core, y = whereabouts()
    tm = lax.axis_index("tm")
    every = range(STREAMS)
    pending = []

    loads = [pltpu.make_async_copy(c_ref, s["cot"], s["load"].at[0])]
    for n in range(LAYERS):
        for k, (name, ref) in enumerate((("wf", wf_ref), ("wg", wg_ref), ("wr", wr_ref))):
            loads.append(pltpu.make_async_copy(ref.at[n], s[name].at[n], s["load"].at[1 + 3 * n + k]))
    for c in loads[1:]:
        c.start()
    loads[0].start()

    def part(ref, q, n):
        return ref.at[pl.ds(q * PART + n * R, R)]

    def moves(kind, n):
        copies = []
        for i in range(4):
            q = (y + i) % 4
            if kind == 0:
                source, target = part(x_ref, q, n), acts.at[0, n, 4 + y]
            elif kind == 1:
                source, target = part(s["cot_b"], q, n), s["top"].at[n, y]
            elif kind == 2:
                source, target = s["final"].at[n, q], part(y_ref, y, n)
            else:
                source, target = s["gain_b"].at[n, q], part(gain_ref, y, n)
            if i == 0:
                copies.append(pltpu.make_async_copy(source, target, s["local"].at[kind, n]))
            else:
                copies.append(
                    send(source, target, s["move_send"].at[kind, n, i - 1], s["move_recv"].at[kind, n, i - 1],
                         device_at(z, x, core, q))
                )
        return copies

    class Move:
        def __init__(self, kind, n):
            self.copies = moves(kind, n)

        def start(self):
            for c in self.copies[1:]:
                c.start()
            self.copies[0].start()
            pending.extend(c.wait_send for c in self.copies[1:])

        def arrived(self):
            self.copies[0].wait()
            for c in self.copies[1:]:
                c.wait_recv()

    def ahead(n, k):
        d = 2**n
        return send(acts.at[n, k, pl.ds(8 - d, d)], acts.at[n, k, pl.ds(4 - d, d)], s["halo_send"].at[0, n, k],
                    s["halo_recv"].at[0, n, k], {"tm": (tm + 1) % 32, "chan": y})

    def behind(n, k):
        d = 2**n
        return send(back.at[n, k, pl.ds(0, d)], back.at[n, k, pl.ds(4, d)], s["halo_send"].at[1, n, k],
                    s["halo_recv"].at[1, n, k], {"tm": (tm + 31) % 32, "chan": y})

    def halo_start(copy, go):
        @pl.when(go)
        def _():
            copy.start()

        def finish():
            @pl.when(go)
            def _():
                copy.wait_send()

        pending.append(finish)

    def halo_wait(copy, go):
        @pl.when(go)
        def _():
            copy.wait_recv()

    @pl.when(tm == 0)
    def _():
        for n in range(LAYERS):
            d = 2**n
            acts[n, :, 4 - d : 4] = jnp.zeros((STREAMS, d, R, C), BF16)

    @pl.when(tm == 31)
    def _():
        for n in range(LAYERS):
            d = 2**n
            back[n, :, 4 : 4 + d] = jnp.zeros((STREAMS, d, R, C), BF16)

    greet()
    enter = [Move(0, k) for k in every]
    top = [Move(1, k) for k in every]
    leave = [Move(2, k) for k in every]
    end = [Move(3, k) for k in every]
    for k in every:
        enter[k].start()

    def columns(step):
        return pl.ds(pl.multiple_of(step * NT, NT), NT)

    def tiles(count):
        return lambda f: pl.loop(0, count)(f)

    def current(n, k):
        return acts[n, k, 4:8].reshape(ROWS, C)

    def delayed(n, k):
        d = 2**n
        return acts[n, k, 4 - d : 8 - d].reshape(ROWS, C)

    def forward_now(n, k):
        @tiles(C // NT)
        def _(t):
            cols = columns(t)
            v = current(n, k)
            s["pre_f"][k, :, cols] = dot(v, s["wf"][n, 1, :, cols])
            s["pre_g"][k, :, cols] = dot(v, s["wg"][n, 1, :, cols])

    def forward_rest(n, k):
        @tiles(C // NT)
        def _(t):
            cols = columns(t)
            v = delayed(n, k)
            f = jnp.tanh(s["pre_f"][k, :, cols] + dot(v, s["wf"][n, 0, :, cols]))
            g = 0.5 + 0.5 * jnp.tanh(0.5 * (s["pre_g"][k, :, cols] + dot(v, s["wg"][n, 0, :, cols])))
            h = f * g
            s["hidden"][n, k, :, cols] = h.astype(BF16)
            s["coef_f"][n, k, :, cols] = g - f * h
            s["coef_g"][n, k, :, cols] = h - h * g

        @tiles(C // NT)
        def _(t):
            cols = columns(t)
            v = acts[n, k, 4:8, :, cols].reshape(ROWS, NT).astype(F32)
            v = (v + dot(s["hidden"][n, k], s["wr"][n, :, cols])).astype(BF16).reshape(4, R, NT)
            if n + 1 < LAYERS:
                acts[n + 1, k, 4:8, :, cols] = v
            else:
                s["final"][k, :, :, cols] = v

    for n in range(LAYERS):
        for k in every:
            if n == 0:
                enter[k].arrived()
                halo_start(ahead(0, k), tm < 31)
                if k == 0:
                    for c in loads[1:4]:
                        c.wait()
            forward_now(n, k)
        if n == 0:
            loads[0].wait()
            s["cot_b"][...] = s["cot"][...].astype(BF16)
            for k in every:
                top[k].start()
        for k in every:
            halo_wait(ahead(n, k), tm > 0)
            forward_rest(n, k)
            if n + 1 < LAYERS:
                halo_start(ahead(n + 1, k), tm < 31)
            else:
                leave[k].start()
        if n + 1 < LAYERS:
            for c in loads[4 + 3 * n : 7 + 3 * n]:
                c.wait()

    def adjoint(n, k):
        if n == LAYERS - 1:
            top[k].arrived()
            return
        d = 2 ** (n + 1)
        s["gain"][k] += back[n + 1, k, d : 4 + d].reshape(ROWS, C).astype(F32)
        s["adj"][k] = (s["gain"][k] + s["top"][k].reshape(ROWS, C).astype(F32)).astype(BF16)

    def gates(n, k):
        @tiles(C // NT)
        def _(t):
            cols = columns(t)
            v = s["top"][k].reshape(ROWS, C) if n == LAYERS - 1 else s["adj"][k]
            dh = dot_nt(v, s["wr"][n, cols, :])
            s["dfg"][0, k, :, cols] = (dh * s["coef_f"][n, k, :, cols]).astype(BF16)
            s["dfg"][1, k, :, cols] = (dh * s["coef_g"][n, k, :, cols]).astype(BF16)

    def both(n, k, tap, rows):
        return dot_nt(s["dfg"][0, k], s["wf"][n, tap, rows, :]) + dot_nt(s["dfg"][1, k], s["wg"][n, tap, rows, :])

    def backward_far(n, k):
        @tiles(C // NT)
        def _(t):
            cols = columns(t)
            back[n, k, 0:4, :, cols] = both(n, k, 0, cols).astype(BF16).reshape(4, R, NT)

    def backward_now(n, k):
        @tiles(C // NT)
        def _(t):
            cols = columns(t)
            if n == LAYERS - 1:
                s["gain"][k, :, cols] = both(n, k, 1, cols)
            else:
                s["gain"][k, :, cols] += both(n, k, 1, cols)

    def weights(n):
        for k in every:
            cols = pl.ds(k * ROWS, ROWS)
            s["flip"][0, :, cols] = delayed(n, k).T
            s["flip"][1, :, cols] = current(n, k).T
            s["flip"][2, :, cols] = s["hidden"][n, k].T

        def store(value, m, t):
            value = value.astype(BF16)
            for j in range(NT // 128):
                grads[n, (NT // 128) * t + j, :, :, :, m * 16 : m * 16 + 16, :] = value[:, j * 128 : j * 128 + 128].reshape(
                    4, 4, 2, 16, 128
                )

        @tiles(C // NT)
        def _(t):
            cols = columns(t)
            for m in range(4):
                d = s["dfg"][m // 2, :, :, cols].reshape(4 * PART, NT)
                store(dot(s["flip"][m % 2], d), m, t)
            if n == LAYERS - 1:
                d = s["top"][:, :, :, cols].reshape(4 * PART, NT)
            else:
                d = s["adj"][:, :, cols].reshape(4 * PART, NT)
            store(dot(s["flip"][2], d), 4, t)

    work = [Reduce(n, grads, out_ref, s) for n in range(LAYERS)]
    for n in reversed(range(LAYERS)):
        for k in every:
            if n + 1 < LAYERS:
                halo_wait(behind(n + 1, k), tm < 31)
            adjoint(n, k)
            gates(n, k)
            if n:
                backward_far(n, k)
                halo_start(behind(n, k), tm > 0)
        if n:
            if n + 1 < LAYERS:
                work[n + 1].step(1)
            for k in every:
                backward_now(n, k)
            if n + 1 < LAYERS:
                work[n + 1].step(2)
            weights(n)
            work[n].step(0)
            if n + 1 < LAYERS:
                work[n + 1].step(3)
        else:
            work[1].step(1)
            weights(0)
            work[0].step(0)
            for k in every:
                backward_far(0, k)
                halo_start(behind(0, k), tm > 0)
            work[0].step(1)
            work[1].step(2)
            for k in every:
                backward_now(0, k)
            for k in every:
                halo_wait(behind(0, k), tm < 31)
                s["gain_b"][k] = (s["gain"][k] + back[0, k, 1:5].reshape(ROWS, C).astype(F32)).astype(BF16).reshape(4, R, C)
                end[k].start()
            work[0].step(2)
            work[1].step(3)
            work[0].step(3)
            work[2].step(4)
            work[1].step(4)
            work[0].step(4)
    for k in every:
        leave[k].arrived()
        end[k].arrived()
    for w in work:
        w.drain()
    for p in pending:
        p()


def body(inputs, cotangent, w_filter, w_gate, w_res):
    anywhere = pl.BlockSpec(memory_space=pl.ANY)
    out, gain, sums = pl.pallas_call(
        pass_kernel,
        out_shape=(
            jax.ShapeDtypeStruct(inputs.shape, BF16),
            jax.ShapeDtypeStruct(inputs.shape, BF16),
            jax.ShapeDtypeStruct((LAYERS, DEEP, 128), F32),
        ),
        in_specs=[anywhere] * 5,
        out_specs=(anywhere, anywhere, pl.BlockSpec(memory_space=pltpu.VMEM)),
        scratch_shapes=list(SCRATCH.values()),
        compiler_params=pltpu.CompilerParams(collective_id=0, has_side_effects=True, vmem_limit_bytes=63 << 20),
        name="training_pass",
    )(inputs, cotangent, w_filter, w_gate, w_res)
    sums = sums.reshape(LAYERS, MATS, 16, 128)
    return (out, cotangent + gain.astype(F32), sums[:, 0:2], sums[:, 2:4], sums[:, 4])


def solution(mesh):
    rows = P(("win", "tm", "chan"), None)
    return jax.shard_map(
        body,
        mesh=mesh,
        in_specs=(rows, rows, P(), P(), P()),
        out_specs=(rows, rows, P("win", None, "tm", "chan"), P("win", None, "tm", "chan"), P("win", "tm", "chan")),
        check_vma=False,
    )
```

time: 1130 us -> 106 us (0.09)
  the two profiles are of different devices: /device:TPU:16 before, /device:TPU:32 now
where the time goes in v2:
time: 106 us
  Pallas kernels  98.8 us (93%)
  local copies, waits for them, and re-layouts  3.67 us (3%)
  other arithmetic  2.53 us (2%)
    pallas_call x1, Pallas kernels, body(): pl.pallas_call(pass_kernel, out_shape=(jax.ShapeDtypeStruct(inputs.shape,...  98.8 us
    add x1, other arithmetic, body(): cotangent + gain.astype(F32)  2.53 us

profile of v2, /device:TPU:32, one launch (start us, length us, event | category | flops | bytes accessed | tf_op | source)
XLA Modules:
  0.0 105.6 jit_solution(10439506582848643093)
XLA Ops:
  0.6 98.8 %training_pass.1 = (bf16[512,512]{1,0:T(8,128)(2,1)}, bf16[512,512]{1,0:T(8,128)(2,1)}, f32[3,80,128]{2,1,0:T(8,128)}) custom-call(bf16[512,512]{1,0:T(8,128)(2,1)} %x_ref.1, f32[512,512]{1,0:T(8,128)} %c_ref.1, bf16[3,2,512,512]{3,2,1,0:T(8,128)(2,1)} %wf_ref.1, bf16[3,2,512,512]{3,2,1,0:T(8,128)(2,1)} %wg_ref.1, bf16[3,512,512]{2,1,0:T(8,128)(2,1)} %wr_ref.1), custom_call_target="tpu_custom_call" | custom-call | tf_op jit(solution)/shard_map/training_pass/pallas_call | solution.py:478
  99.4 0.0 copy-start
  99.4 1.4 %slice_bitcast_fusion = f32[3,16,128]{2,1,0:T(8,128)} fusion(f32[3,5,16,128]{3,2,1,0:T(8,128)} %bitcast.5), kind=kLoop, calls=%fused_computation.1 | loop fusion | bytes 49152 | tf_op jit(solution)/shard_map/squeeze | solution.py:492
  100.8 1.5 %fusion = (f32[3,2,16,128]{3,2,1,0:T(8,128)}, f32[3,2,16,128]{3,2,1,0:T(8,128)}) fusion(f32[3,5,16,128]{3,2,1,0:T(8,128)} %bitcast.6), kind=kLoop, calls=%fused_computation.2 | loop fusion | bytes 196608 | tf_op jit(solution)/shard_map/slice | solution.py:492
  102.3 2.5 %convert_add_fusion = f32[512,512]{1,0:T(8,128)} fusion(f32[512,512]{1,0:T(8,128)} %c_ref.1, bf16[512,512]{1,0:T(8,128)(2,1)} %get-tuple-element.9), kind=kLoop, calls=%fused_computation | loop fusion | flops 524288 | bytes 2621440 | tf_op jit(solution)/shard_map/add | solution.py:492
  104.8 0.0 copy-done
  104.8 0.8 copy.13
Async XLA Ops:
  99.4 5.4 %copy-start = (bf16[512,512]{1,0:T(8,128)(2,1)S(1)}, bf16[512,512]{1,0:T(8,128)(2,1)}, u32[]{:S(2)}) copy-start(bf16[512,512]{1,0:T(8,128)(2,1)} %get-tuple-element.18) | copy-start | bytes 1572868
